TPU v7x, 256 devices: a whole 4x4x8 slice. The times are simulated.
256 devices in a mesh: pipe: 16 (over z_lo, x, core), ctx: 16 (over y, z_hi).
Axes of the slice: x: 4, y: 4, z: 8 (z_hi: 4, z_lo: 2; z = z_hi * 2 + z_lo), core: 2. Of those that a mesh axis runs over, the one named last changes fastest.
Arguments:
- queries: bfloat16 [2, 16, 2048, 2560], P(None, 'pipe', 'ctx'), may hold values from -80 to 80
- keys: bfloat16 [2, 16, 2048, 512], P(None, 'pipe', 'ctx'), may hold values from -25 to 25
- values: bfloat16 [2, 16, 2048, 512], P(None, 'pipe', 'ctx'), may hold values from -6 to 6
- grad_a: bfloat16 [16, 2048, 2560], P('pipe', 'ctx'), may hold values from -96 to 96
- grad_b: bfloat16 [16, 2048, 2560], P('pipe', 'ctx'), may hold values from -48 to 48
- imports: int32 [2, 16, 16, 16], P(None, 'pipe'), may hold values from 0 to 1, as said below
- block_ids: int32 [2, 16, 16], P(None, 'pipe'), may hold values from 0 to 15, each once within a row
Outputs:
- dq_a: bfloat16 [16, 2048, 2560], P('pipe', 'ctx')
- dq_b: bfloat16 [16, 2048, 2560], P('pipe', 'ctx')
- kv_grads: bfloat16 [2, 16, 2048, 1024], P(None, 'pipe', 'ctx')
Inputs may be any that keep to these rules, and one draw needn't show every extreme that they name: Every file block sees itself and imports at most 7 other blocks; in each micro-batch and section some block imports exactly 7.
All inputs are finite; a program needn't handle non-finite values.
Results may differ from a plain program's by a relative error of at most 0.015.
Values may be sent and summed in bfloat16 or wider, within the bound.
A program may use at most 64 MiB of HBM per device.

v0:
```python
import math
import jax
import jax.numpy as jnp
from jax import lax
from jax.sharding import PartitionSpec as P

QUERY_HEADS = 20
KEY_VALUE_HEADS = 4
HEAD_DIMENSION = 128
FILE_BLOCK_SIZE = 128
MICRO_BATCHES = 2
negative_large = -1e30


def passed_along(block, axis, distance):
    devices = range(lax.axis_size(axis))
    route = [(i - distance, i) for i in devices if i - distance in devices]
    return lax.ppermute(block, axis, route)


def slot_table(import_mask, block_order):
    blocks_all = block_order.shape[0]
    onehot = (block_order[:, None] == jnp.arange(blocks_all, dtype=jnp.int32)[None, :]).astype(
        jnp.float32
    )
    mapped = jnp.dot(onehot, import_mask.astype(jnp.float32), precision=lax.Precision.HIGHEST)
    return jnp.dot(mapped, onehot.T, precision=lax.Precision.HIGHEST)


def frame_setup(slot_mask, query_start, row_total):
    row_index = query_start + jnp.arange(row_total, dtype=jnp.int32)
    query_slots = row_index // FILE_BLOCK_SIZE
    onehot = (
        query_slots[:, None] == jnp.arange(slot_mask.shape[0], dtype=jnp.int32)[None, :]
    ).astype(jnp.float32)
    reachable = jnp.dot(onehot, slot_mask, precision=lax.Precision.HIGHEST)
    return (reachable, query_slots, row_index % FILE_BLOCK_SIZE)


def tile_mask(frame_info, key_start, key_total_count):
    reachable, query_slots, query_place = frame_info
    key_index = key_start + jnp.arange(key_total_count, dtype=jnp.int32)
    key_slots = key_index // FILE_BLOCK_SIZE
    onehot_keys = (
        key_slots[:, None] == jnp.arange(reachable.shape[1], dtype=jnp.int32)[None, :]
    ).astype(jnp.float32)
    allowed_slot = jnp.dot(reachable, onehot_keys.T, precision=lax.Precision.HIGHEST) > 0.5
    same_slot = query_slots[:, None] == key_slots[None, :]
    causal = (key_index % FILE_BLOCK_SIZE)[None, :] <= query_place[:, None]
    return allowed_slot & (jnp.logical_not(same_slot) | causal)


def over_piece(step_fn, carried, pieces):
    key_fragment, value_fragment = pieces
    piece_rows = key_fragment.shape[0]

    def loop_turn(turn_index, carry_state):
        key_block = lax.dynamic_slice_in_dim(
            key_fragment, turn_index * FILE_BLOCK_SIZE, FILE_BLOCK_SIZE, 0
        )
        value_block = lax.dynamic_slice_in_dim(
            value_fragment, turn_index * FILE_BLOCK_SIZE, FILE_BLOCK_SIZE, 0
        )
        return step_fn(carry_state, key_block, value_block, turn_index * FILE_BLOCK_SIZE)

    return lax.fori_loop(0, piece_rows // FILE_BLOCK_SIZE, loop_turn, carried)


def micro_pass(query_row_tensor, key_rows, value_rows, incoming_gradient, slot_mask, query_start):
    row_total = query_row_tensor.shape[0]
    query_group_width = QUERY_HEADS // KEY_VALUE_HEADS
    softmax_scale = 1.0 / math.sqrt(HEAD_DIMENSION)
    query_head_tensor = query_row_tensor.reshape(
        row_total, KEY_VALUE_HEADS, query_group_width, HEAD_DIMENSION
    )
    gradient_heads = incoming_gradient.reshape(
        row_total, KEY_VALUE_HEADS, query_group_width, HEAD_DIMENSION
    )
    frame_info = frame_setup(slot_mask, query_start, row_total)
    overall_rows = slot_mask.shape[0] * FILE_BLOCK_SIZE

    def stat_step(carried, key_fragment, value_fragment, key_start):
        key_total_count = key_fragment.shape[0]
        allowed = tile_mask(frame_info, key_start, key_total_count)

        def stat_compute_tile(carry_state):
            running_max, running_sum, weighted = carry_state
            key_head_tensor = key_fragment.reshape(key_total_count, KEY_VALUE_HEADS, HEAD_DIMENSION)
            value_head_tensor = value_fragment.reshape(
                key_total_count, KEY_VALUE_HEADS, HEAD_DIMENSION
            )
            scores = (
                jnp.einsum(
                    "rhgd,khd->hgrk",
                    query_head_tensor,
                    key_head_tensor,
                    preferred_element_type=jnp.float32,
                )
                * softmax_scale
            )
            masked = jnp.where(allowed, scores, negative_large)
            new_max = jnp.maximum(running_max, jnp.max(masked, axis=-1))
            weights = jnp.where(allowed, jnp.exp(masked - new_max[..., None]), 0.0)
            rescale = jnp.exp(running_max - new_max)
            running_sum = running_sum * rescale + jnp.sum(weights, axis=-1)
            added = jnp.einsum(
                "hgrk,khd->rhgd",
                weights.astype(jnp.bfloat16),
                value_head_tensor,
                preferred_element_type=jnp.float32,
            )
            weighted = weighted * jnp.transpose(rescale, (2, 0, 1))[..., None] + added
            return (new_max, running_sum, weighted)

        return lax.cond(
            jnp.any(allowed), stat_compute_tile, lambda carry_state: carry_state, carried
        )

    stat_start = (
        jnp.full((KEY_VALUE_HEADS, query_group_width, row_total), negative_large, jnp.float32),
        jnp.zeros((KEY_VALUE_HEADS, query_group_width, row_total), jnp.float32),
        jnp.zeros((row_total, KEY_VALUE_HEADS, query_group_width, HEAD_DIMENSION), jnp.float32),
    )
    stats = over_piece(
        stat_step,
        stat_start,
        (
            lax.all_gather(key_rows, "ctx", axis=0, tiled=True),
            lax.all_gather(value_rows, "ctx", axis=0, tiled=True),
        ),
    )
    running_max, running_sum, weighted = stats
    attended = weighted / jnp.transpose(running_sum, (2, 0, 1))[..., None]
    log_total = running_max + jnp.log(running_sum)
    delta = jnp.transpose(
        jnp.sum(gradient_heads.astype(jnp.float32) * attended, axis=-1), (1, 2, 0)
    )

    def grad_step(carried, key_fragment, value_fragment, key_start):
        key_total_count = key_fragment.shape[0]
        allowed = tile_mask(frame_info, key_start, key_total_count)

        def grad_compute_tile(carry_state):
            q_grad, kv_sums = carry_state
            key_head_tensor = key_fragment.reshape(key_total_count, KEY_VALUE_HEADS, HEAD_DIMENSION)
            value_head_tensor = value_fragment.reshape(
                key_total_count, KEY_VALUE_HEADS, HEAD_DIMENSION
            )
            scores = (
                jnp.einsum(
                    "rhgd,khd->hgrk",
                    query_head_tensor,
                    key_head_tensor,
                    preferred_element_type=jnp.float32,
                )
                * softmax_scale
            )
            probs = jnp.where(
                allowed,
                jnp.exp(jnp.where(allowed, scores - log_total[..., None], negative_large)),
                0.0,
            )
            value_gradient = jnp.einsum(
                "hgrk,rhgd->khd",
                probs.astype(jnp.bfloat16),
                gradient_heads,
                preferred_element_type=jnp.float32,
            )
            prob_grad = jnp.einsum(
                "rhgd,khd->hgrk",
                gradient_heads,
                value_head_tensor,
                preferred_element_type=jnp.float32,
            )
            score_grad = (probs * (prob_grad - delta[..., None])).astype(jnp.bfloat16)
            q_grad = q_grad + jnp.einsum(
                "hgrk,khd->rhgd", score_grad, key_head_tensor, preferred_element_type=jnp.float32
            )
            key_gradient = (
                jnp.einsum(
                    "hgrk,rhgd->khd",
                    score_grad,
                    query_head_tensor,
                    preferred_element_type=jnp.float32,
                )
                * softmax_scale
            )
            update_rows = jnp.concatenate(
                [
                    key_gradient.reshape(key_total_count, KEY_VALUE_HEADS * HEAD_DIMENSION),
                    value_gradient.reshape(key_total_count, KEY_VALUE_HEADS * HEAD_DIMENSION),
                ],
                axis=1,
            )
            previous = lax.dynamic_slice_in_dim(kv_sums, key_start, key_total_count, 0)
            kv_sums = lax.dynamic_update_slice_in_dim(kv_sums, previous + update_rows, key_start, 0)
            return (q_grad, kv_sums)

        return lax.cond(
            jnp.any(allowed), grad_compute_tile, lambda carry_state: carry_state, carried
        )

    grad_start = (
        jnp.zeros((row_total, KEY_VALUE_HEADS, query_group_width, HEAD_DIMENSION), jnp.float32),
        jnp.zeros((overall_rows, 2 * KEY_VALUE_HEADS * HEAD_DIMENSION), jnp.float32),
    )
    q_grad, kv_sums = over_piece(
        grad_step,
        grad_start,
        (
            lax.all_gather(key_rows, "ctx", axis=0, tiled=True),
            lax.all_gather(value_rows, "ctx", axis=0, tiled=True),
        ),
    )
    returned = lax.psum_scatter(
        kv_sums.astype(jnp.bfloat16), "ctx", scatter_dimension=0, tiled=True
    )
    q_result = (
        (q_grad * softmax_scale)
        .reshape(row_total, QUERY_HEADS * HEAD_DIMENSION)
        .astype(jnp.bfloat16)
    )
    return (q_result, returned)


def on_device(queries, keys, values, grad_a, grad_b, imports, block_ids):
    row_total = queries.shape[2]
    query_start = lax.axis_index("ctx") * row_total
    outputs = []
    kv_results = []
    incoming_gradient = grad_a[0]
    for micro_index in range(MICRO_BATCHES):
        if micro_index > 0:
            arrived = passed_along(outputs[0], "pipe", -1)
            incoming_gradient = (
                grad_b[0].astype(jnp.float32) + arrived.astype(jnp.float32)
            ).astype(jnp.bfloat16)
        slot_mask = slot_table(imports[micro_index, 0], block_ids[micro_index, 0])
        q_result, kv_result = micro_pass(
            queries[micro_index, 0],
            keys[micro_index, 0],
            values[micro_index, 0],
            incoming_gradient,
            slot_mask,
            query_start,
        )
        outputs.append(q_result)
        kv_results.append(kv_result)
    return (outputs[0][None], outputs[1][None], jnp.stack(kv_results)[:, None])


def solution(mesh):
    return jax.shard_map(
        on_device,
        mesh=mesh,
        in_specs=(
            P(None, "pipe", "ctx", None),
            P(None, "pipe", "ctx", None),
            P(None, "pipe", "ctx", None),
            P("pipe", "ctx", None),
            P("pipe", "ctx", None),
            P(None, "pipe", None, None),
            P(None, "pipe", None),
        ),
        out_specs=(P("pipe", "ctx", None), P("pipe", "ctx", None), P(None, "pipe", "ctx", None)),
        check_vma=False,
    )
```

profile of v0, /device:TPU:4, one launch (start us, length us, event | category | flops | bytes accessed | tf_op | source)
XLA Modules:
  0.0 529.2 jit_solution(5274312944231669213)
XLA Ops:
  7.2 1.0 fusion.103
  9.1 1.0 fusion.102
  14.2 1.1 copy.67
  15.3 1.4 fusion.101
  17.0 1.1 copy.66
  18.4 1.1 copy.59
  19.5 56.7 %all-gather.9.cloned.1.call-done = bf16[1,1,2048,512]{2,3,1,0:T(8,128)(2,1)} async-done(((bf16[1,1,128,512]{2,3,1,0:T(8,128)(2,1)}), bf16[1,1,2048,512]{2,3,1,0:T(8,128)(2,1)}) %all-gather.9.cloned.1.call-update) | async-done | bytes 2097168 | tf_op jit(solution)/shard_map/all_gather | solution.py:211
  76.2 62.1 %all-gather.11.cloned.1.call-done = bf16[1,1,2048,512]{2,3,1,0:T(8,128)(2,1)} async-done(((bf16[1,1,128,512]{2,3,1,0:T(8,128)(2,1)}), bf16[1,1,2048,512]{2,3,1,0:T(8,128)(2,1)}) %all-gather.11.cloned.1.call-update) | async-done | bytes 2097168 | tf_op jit(solution)/shard_map/all_gather | solution.py:212
  138.4 40.5 %while.80 = (s32[]{:T(128)}, f32[4,5,128]{2,1,0:T(8,128)S(1)}, f32[4,5,128]{2,1,0:T(8,128)S(1)}, f32[128,4,5,128]{3,0,2,1:T(8,128)S(1)}, f32[128,16]{0,1:T(8,128...) while((s32[]{:T(128)}, f32[4,5,128]{2,1,0:T(8,128)S(1)}, ...), condition=%wide.region_6.7_spmd.clone.clone, body=%wide.region_0.6_spmd.clone.clone.sunk | while | flops 174651904 | bytes 8237349 | solution.py:66
  140.0 3.7 conditional.16
  140.0 1.0 constant_dynamic-slice_fusion
  141.0 1.5 fusion.95
  143.8 0.9 fusion.145
  145.4 0.9 fusion.145
  147.0 0.9 fusion.145
  150.2 0.9 fusion.145
  151.7 3.7 conditional.16
  151.8 1.0 constant_dynamic-slice_fusion
  152.8 1.5 fusion.95
  155.5 0.9 fusion.145
  158.7 0.9 fusion.145
  163.5 0.9 fusion.145
  166.7 3.7 conditional.16
  166.7 1.0 constant_dynamic-slice_fusion
  167.7 1.5 fusion.95
  175.2 3.7 conditional.16
  175.2 1.0 constant_dynamic-slice_fusion
  176.2 1.5 fusion.95
  179.0 1.5 copy.61
  180.4 1.5 multiply_reduce_fusion.1
  182.1 4.3 broadcast.931.clone
  186.5 46.3 %while.81 = (s32[]{:T(128)}, f32[128,4,5,128]{3,0,2,1:T(8,128)S(1)}, f32[2048,1024]{0,1:T(8,128)}, f32[128,16]{0,1:T(8,128)S(1)}, bf16[2048,512]{0,1:T(8,128)(2,...) while((s32[]{:T(128)}, ...), condition=%wide.region_12.13_spmd.clone.clone, body=%wide.region_8.12_spmd.clone.clone.sunk | while | flops 425974784 | bytes 14221625 | solution.py:66
  188.0 5.2 conditional.17
  188.0 1.0 constant_dynamic-slice_fusion.2
  191.3 2.0 fusion.39
  201.2 5.2 conditional.17
  201.2 1.0 constant_dynamic-slice_fusion.2
  204.4 2.0 fusion.39
  217.5 5.2 conditional.17
  217.5 1.0 constant_dynamic-slice_fusion.2
  220.8 2.0 fusion.39
  227.5 5.2 conditional.17
  227.5 1.0 constant_dynamic-slice_fusion.2
  230.7 2.0 fusion.39
  232.7 1.5 copy.62
  234.2 2.4 multiply_convert_fusion.1
  236.6 1.9 collective-permute-start
  238.6 24.7 %all-gather.15.cloned.1.call-done = bf16[1,1,2048,512]{2,3,1,0:T(8,128)(2,1)} async-done(((bf16[1,1,128,512]{2,3,1,0:T(8,128)(2,1)}), bf16[1,1,2048,512]{2,3,1,0:T(8,128)(2,1)}) %all-gather.15.cloned.1.call-update) | async-done | bytes 2097168 | tf_op jit(solution)/shard_map/all_gather | solution.py:212
  263.4 28.2 %while.82 = (s32[]{:T(128)}, f32[4,5,128]{2,1,0:T(8,128)S(1)}, f32[4,5,128]{2,1,0:T(8,128)S(1)}, f32[128,4,5,128]{3,0,2,1:T(8,128)S(1)}, f32[128,16]{0,1:T(8,128...) while((s32[]{:T(128)}, f32[4,5,128]{2,1,0:T(8,128)S(1)}, ...), condition=%wide.region_19.20_spmd.clone.clone, body=%wide.region_13.0_spmd.clone.clone.sunk | while | flops 174651904 | bytes 8237349 | solution.py:66
  265.0 2.6 conditional.18
  265.0 1.0 constant_dynamic-slice_fusion.4
  292.0 7.3 %copy.70 = bf16[2048,1024]{1,0:T(8,128)(2,1)} copy(f32[2048,1024]{0,1:T(8,128)} %get-tuple-element.1589) | data formatting | bytes 12582912 | tf_op jit(solution)/shard_map/while | solution.py:66
  300.4 1.3 fusion.76
  302.0 4.3 broadcast.931
  306.4 30.7 %while.83 = (s32[]{:T(128)}, f32[128,4,5,128]{3,0,2,1:T(8,128)S(1)}, f32[2048,1024]{0,1:T(8,128)}, f32[128,16]{0,1:T(8,128)S(1)}, bf16[2048,512]{0,1:T(8,128)(2,...) while((s32[]{:T(128)}, ...), condition=%wide.region_25.26_spmd.clone.clone, body=%wide.region_21.25_spmd.clone.clone.sunk | while | flops 425974784 | bytes 14221625 | solution.py:66
  307.9 5.2 conditional.19
  307.9 1.0 constant_dynamic-slice_fusion.6
  311.2 2.0 fusion.63
  337.1 7.3 %copy.71 = bf16[2048,1024]{1,0:T(8,128)(2,1)} copy(f32[2048,1024]{0,1:T(8,128)} %get-tuple-element.1590) | data formatting | bytes 12582912 | tf_op jit(solution)/shard_map/while | solution.py:66
  344.4 2.2 copy.72
  347.2 1.1 copy.73
  348.3 73.8 %reduce-scatter.3.cloned.1.call-done = bf16[128,1024]{1,0:T(8,128)(2,1)} async-done(((bf16[2048,1024]{1,0:T(8,128)(2,1)}), bf16[128,1024]{1,0:T(8,128)(2,1)}) %reduce-scatter.3.cloned.1.call-update) | async-done | bytes 262160 | tf_op jit(solution)/shard_map/reduce_scatter | solution.py:215
  422.0 98.4 %reduce-scatter.5.cloned.1.call-done = bf16[128,1024]{1,0:T(8,128)(2,1)} async-done(((bf16[2048,1024]{1,0:T(8,128)(2,1)}), bf16[128,1024]{1,0:T(8,128)(2,1)}) %reduce-scatter.5.cloned.1.call-update) | async-done | bytes 262160 | tf_op jit(solution)/shard_map/reduce_scatter | solution.py:215
  520.5 1.9 maximum_bitcast_fusion
  (345 shorter events, 77.5 us)
Async XLA Ops:
  7.2 5.4 %copy-start.4 = (s32[2,1,16]{2,1,0:T(1,128)S(1)}, s32[2,1,16]{2,1,0:T(1,128)}, u32[]{:S(2)}) copy-start(s32[2,1,16]{2,1,0:T(1,128)} %param.29) | copy-start | bytes 388
  7.2 5.4 %copy-start.5 = (s32[2,1,16,16]{3,2,1,0:T(8,128)S(1)}, s32[2,1,16,16]{3,2,1,0:T(8,128)}, u32[]{:S(2)}) copy-start(s32[2,1,16,16]{3,2,1,0:T(8,128)} %param.28) | copy-start | bytes 6148
  7.2 69.0 %all-gather.9.cloned.1.call-start = ((), (), s32[]{:S(2)}) async-start(), calls=%async_computation.4 | async-start | bytes 2228224 | tf_op jit(solution)/shard_map/all_gather | solution.py:211
  8.2 5.6 %copy-start.2 = (bf16[1,128,2560]{2,1,0:T(8,128)(2,1)S(1)}, bf16[1,128,2560]{2,1,0:T(8,128)(2,1)}, u32[]{:S(2)}) copy-start(bf16[1,128,2560]{2,1,0:T(8,128)(2,1)} %param.26) | copy-start | bytes 1966084
  9.0 129.3 %all-gather.11.cloned.1.call-start = ((), (), s32[]{:S(2)}) async-start(), calls=%async_computation.5 | async-start | bytes 2228224 | tf_op jit(solution)/shard_map/all_gather | solution.py:212
  10.8 3.4 copy-start.3
  10.8 227.7 %all-gather.13.cloned.1.call-start = ((), (), s32[]{:S(2)}) async-start(), calls=%async_computation.6 | async-start | bytes 2228224 | tf_op jit(solution)/shard_map/all_gather | solution.py:211
  11.7 251.6 %all-gather.15.cloned.1.call-start = ((), (), s32[]{:S(2)}) async-start(), calls=%async_computation.7 | async-start | bytes 2228224 | tf_op jit(solution)/shard_map/all_gather | solution.py:212
  12.5 409.6 %reduce-scatter.3.cloned.1.call-start = ((), (), s32[]{:S(2)}) async-start(), calls=%async_computation.2 | async-start | bytes 4456448 | tf_op jit(solution)/shard_map/reduce_scatter | solution.py:215
  234.2 29.2 %copy-start = (bf16[128,4,5,128]{3,0,2,1:T(8,128)(2,1)S(1)}, bf16[128,4,5,128]{3,0,2,1:T(8,128)(2,1)}, u32[]{:S(2)}) copy-start(bf16[128,4,5,128]{3,0,2,1:T(8,128)(2,1)} %copy.66) | copy-start | bytes 1966084
  236.6 63.0 %collective-permute-start = (bf16[128,2560]{0,1:T(8,128)(2,1)}, bf16[128,2560]{0,1:T(8,128)(2,1)}, u32[]{:S(2)}, u32[]{:S(2)}) collective-permute-start(bf16[128,2560]{0,1:T(8,128)(2,1)} %bitcast.61), channel_id=1, source_target_pairs={{16,0},{32,16},{48,32},{64,48},{80,64},{96,80},{112,96},{128,112},... | collective-permute-start | bytes 1966088 | tf_op jit(solution)/shard_map/ppermute | solution.py:18
  299.3 1.1 copy-start.1
  299.3 221.1 %reduce-scatter.5.cloned.1.call-start = ((), (), s32[]{:S(2)}) async-start(), calls=%async_computation.3 | async-start | bytes 4456448 | tf_op jit(solution)/shard_map/reduce_scatter | solution.py:215
Sparse Core Ops, SparseCore 0:
  11.0 65.1 all-gather.8
  78.6 59.6 all-gather.10
  140.7 59.8 all-gather.12
  202.8 60.3 all-gather.14
  299.5 122.5 reduce-scatter.2
  425.5 94.8 reduce-scatter.4
where the time goes:
time: 532 us; the launch traced here: 529 us
  waiting for transfers between devices  316 us (59%)
  matrix products  79 us (15%)
  local copies, waits for them, and re-layouts  52.4 us (10%)
  loops' own time  45.2 us (8%)
  other arithmetic  20.2 us (4%)
  between operations  14.4 us (3%)
    reduce_scatter x2, waiting for transfers between devices, micro_pass(): lax.psum_scatter(kv_sums.astype(jnp.bfloat16), 'ctx', scatter_dimension=0...  172 us
    all_gather x2, waiting for transfers between devices, micro_pass(): lax.all_gather(value_rows, 'ctx', axis=0, tiled=True)  86.8 us
    all_gather x2, waiting for transfers between devices, micro_pass(): lax.all_gather(key_rows, 'ctx', axis=0, tiled=True)  56.7 us
    dot_general x64, matrix products, tile_mask(): jnp.dot(reachable, onehot_keys.T, precision=lax.Precision.HIGHEST) > 0.5  55.8 us
    another operation x4, loops' own time, over_piece(): return lax.fori_loop(0, piece_rows // FILE_BLOCK_SIZE, loop_turn, carried)  43.8 us
    while x6, local copies, waits for them, and re-layouts, over_piece(): return lax.fori_loop(0, piece_rows // FILE_BLOCK_SIZE, loop_turn, carried)  18.5 us
    unnamed x22, local copies, waits for them, and re-layouts  10.7 us
  transfers between devices with their start and end apart: 7, of which 5 were waited for; matrix products, arithmetic and copies ran while one was open for 28% of the time, Pallas kernels for 0%

commit v1 on v0

--- a/solution.py
+++ b/solution.py
@@ -208,7 +208,9 @@
         grad_step,
         grad_start,
         (
-            lax.all_gather(key_rows, "ctx", axis=0, tiled=True),
+            jnp.concatenate(
+                lax.all_to_all(jnp.stack([key_rows] * lax.axis_size("ctx")), "ctx", 0, 0), axis=0
+            ),
             lax.all_gather(value_rows, "ctx", axis=0, tiled=True),
         ),
     )

time: 532 us -> 578 us (1.086)
  starting transfers between devices: 2.34 us -> 32.5 us
  local copies, waits for them, and re-layouts: 52.4 us -> 70.5 us
    all_to_all x0 -> x2, starting transfers between devices: none -> 30.2 us  [micro_pass(): lax.all_to_all(jnp.stack([key_rows] * lax.axis_size('ctx')), 'ctx', 0, 0)]
    reduce_scatter x2, waiting for transfers between devices: 172 us -> 161 us  [micro_pass(): lax.psum_scatter(kv_sums.astype(jnp.bfloat16), 'ctx', scatter_dimension=0...]
    all_gather x2, waiting for transfers between devices: 56.7 us -> 67.1 us  [micro_pass(): lax.all_gather(key_rows, 'ctx', axis=0, tiled=True)]
    unnamed x22 -> x32, local copies, waits for them, and re-layouts: 10.7 us -> 17.6 us
    all_to_all x0 -> x2, local copies, waits for them, and re-layouts: none -> 6.79 us  [micro_pass(): lax.all_to_all(jnp.stack([key_rows] * lax.axis_size('ctx')), 'ctx', 0, 0)]
    another operation x10 -> x12, local copies, waits for them, and re-layouts: 9.18 us -> 12.7 us
  transfers between devices with their start and end apart: 7 -> 9, of which waited for: 5 -> 5; matrix products, arithmetic and copies ran while one was open for 28% -> 29% of each run, Pallas kernels for 0% -> 0%
where the time goes in v1:
time: 578 us; the launch traced here: 575 us
  waiting for transfers between devices  313 us (54%)
  matrix products  79.6 us (14%)
  local copies, waits for them, and re-layouts  70.5 us (12%)
  loops' own time  45.9 us (8%)
  starting transfers between devices  32.5 us (6%)
  other arithmetic  18.8 us (3%)
  between operations  14.4 us (2%)
    reduce_scatter x2, waiting for transfers between devices, micro_pass(): lax.psum_scatter(kv_sums.astype(jnp.bfloat16), 'ctx', scatter_dimension=0...  161 us
    all_gather x2, waiting for transfers between devices, micro_pass(): lax.all_gather(value_rows, 'ctx', axis=0, tiled=True)  84.7 us
    all_gather x2, waiting for transfers between devices, micro_pass(): lax.all_gather(key_rows, 'ctx', axis=0, tiled=True)  67.1 us
    dot_general x64, matrix products, tile_mask(): jnp.dot(reachable, onehot_keys.T, precision=lax.Precision.HIGHEST) > 0.5  56.5 us
    another operation x4, loops' own time, over_piece(): return lax.fori_loop(0, piece_rows // FILE_BLOCK_SIZE, loop_turn, carried)  44.4 us
    all_to_all x2, starting transfers between devices, micro_pass(): lax.all_to_all(jnp.stack([key_rows] * lax.axis_size('ctx')), 'ctx', 0, 0)  30.2 us
    while x6, local copies, waits for them, and re-layouts, over_piece(): return lax.fori_loop(0, piece_rows // FILE_BLOCK_SIZE, loop_turn, carried)  19.4 us
    unnamed x32, local copies, waits for them, and re-layouts  17.6 us
  transfers between devices with their start and end apart: 9, of which 5 were waited for; matrix products, arithmetic and copies ran while one was open for 29% of the time, Pallas kernels for 0%

profile of v1, /device:TPU:4, one launch (start us, length us, event | category | flops | bytes accessed | tf_op | source)
XLA Modules:
  0.0 575.2 jit_solution(6376369731054151769)
XLA Ops:
  9.0 1.0 fusion.102
  11.7 1.8 stack.15
  13.5 11.4 %all-to-all-start = ((bf16[16,128,512]{1,2,0:T(8,128)(2,1)}), bf16[16,128,512]{1,2,0:T(8,128)(2,1)}, u32[]{:S(2)}, u32[]{:S(2)}) async-start(bf16[16,128,512]{1,2,0:T(8,128)(2,1)} %stack.15), calls=%async_computation | async-start | bytes 4194304 | tf_op jit(solution)/shard_map/all_to_all | solution.py:212
  27.4 1.1 copy.150
  28.5 1.4 fusion.101
  30.2 1.1 copy.149
  31.6 1.1 copy.140
  32.7 67.1 %all-gather.9.cloned.1.call-done = bf16[1,1,2048,512]{2,3,1,0:T(8,128)(2,1)} async-done(((bf16[1,1,128,512]{2,3,1,0:T(8,128)(2,1)}), bf16[1,1,2048,512]{2,3,1,0:T(8,128)(2,1)}) %all-gather.9.cloned.1.call-update) | async-done | bytes 2097168 | tf_op jit(solution)/shard_map/all_gather | solution.py:128
  99.8 62.2 %all-gather.11.cloned.1.call-done = bf16[1,1,2048,512]{2,3,1,0:T(8,128)(2,1)} async-done(((bf16[1,1,128,512]{2,3,1,0:T(8,128)(2,1)}), bf16[1,1,2048,512]{2,3,1,0:T(8,128)(2,1)}) %all-gather.11.cloned.1.call-update) | async-done | bytes 2097168 | tf_op jit(solution)/shard_map/all_gather | solution.py:214
  162.1 41.8 %while.80 = (s32[]{:T(128)}, f32[4,5,128]{2,1,0:T(8,128)S(1)}, f32[4,5,128]{2,1,0:T(8,128)S(1)}, f32[128,4,5,128]{3,0,2,1:T(8,128)S(1)}, f32[128,16]{0,1:T(8,128...) while((s32[]{:T(128)}, f32[4,5,128]{2,1,0:T(8,128)S(1)}, ...), condition=%wide.region_6.7_spmd.clone.clone, body=%wide.region_0.6_spmd.clone.clone.sunk | while | flops 174651904 | bytes 8237349 | solution.py:66
  163.8 3.7 conditional.16
  163.8 1.0 constant_dynamic-slice_fusion
  164.8 1.5 fusion.95
  175.9 3.7 conditional.16
  176.0 1.0 constant_dynamic-slice_fusion
  177.0 1.5 fusion.95
  191.5 3.7 conditional.16
  191.5 1.0 constant_dynamic-slice_fusion
  192.5 1.5 fusion.95
  200.2 3.7 conditional.16
  200.2 1.0 constant_dynamic-slice_fusion
  201.2 1.5 fusion.95
  204.0 1.5 copy.142
  205.4 1.8 stack.16
  207.2 18.8 %all-to-all-start.1 = ((bf16[16,128,512]{1,2,0:T(8,128)(2,1)}), bf16[16,128,512]{1,2,0:T(8,128)(2,1)}, u32[]{:S(2)}, u32[]{:S(2)}) async-start(bf16[16,128,512]{1,2,0:T(8,128)(2,1)} %stack.16), calls=%async_computation.1 | async-start | bytes 4194304 | tf_op jit(solution)/shard_map/all_to_all | solution.py:212
  226.1 3.9 copy.137
  230.0 4.1 copy.143
  234.5 4.3 broadcast.933.clone
  238.8 46.2 %while.81 = (s32[]{:T(128)}, f32[128,4,5,128]{3,0,2,1:T(8,128)S(1)}, f32[2048,1024]{0,1:T(8,128)}, f32[128,16]{0,1:T(8,128)S(1)}, bf16[2048,512]{0,1:T(8,128)(2,...) while((s32[]{:T(128)}, ...), condition=%wide.region_12.13_spmd.clone.clone, body=%wide.region_8.12_spmd.clone.clone.sunk | while | flops 425974784 | bytes 14221625 | solution.py:66
  240.3 5.2 conditional.17
  240.4 1.0 constant_dynamic-slice_fusion.2
  243.6 2.0 fusion.39
  253.5 5.2 conditional.17
  253.5 1.0 constant_dynamic-slice_fusion.2
  256.8 1.9 fusion.39
  269.8 5.2 conditional.17
  269.9 1.0 constant_dynamic-slice_fusion.2
  273.1 2.0 fusion.39
  279.8 5.2 conditional.17
  279.8 1.0 constant_dynamic-slice_fusion.2
  283.1 2.0 fusion.39
  285.0 1.5 copy.144
  286.5 2.4 multiply_convert_fusion.1
  288.9 2.1 collective-permute-start
  291.0 22.5 %all-gather.15.cloned.1.call-done = bf16[1,1,2048,512]{2,3,1,0:T(8,128)(2,1)} async-done(((bf16[1,1,128,512]{2,3,1,0:T(8,128)(2,1)}), bf16[1,1,2048,512]{2,3,1,0:T(8,128)(2,1)}) %all-gather.15.cloned.1.call-update) | async-done | bytes 2097168 | tf_op jit(solution)/shard_map/all_gather | solution.py:214
  313.6 28.2 %while.82 = (s32[]{:T(128)}, f32[4,5,128]{2,1,0:T(8,128)S(1)}, f32[4,5,128]{2,1,0:T(8,128)S(1)}, f32[128,4,5,128]{3,0,2,1:T(8,128)S(1)}, f32[128,16]{0,1:T(8,128...) while((s32[]{:T(128)}, f32[4,5,128]{2,1,0:T(8,128)S(1)}, ...), condition=%wide.region_19.20_spmd.clone.clone, body=%wide.region_13.0_spmd.clone.clone.sunk | while | flops 174651904 | bytes 8237349 | solution.py:66
  315.2 2.6 conditional.18
  315.2 1.0 constant_dynamic-slice_fusion.4
  341.8 1.5 copy.151
  343.3 2.9 copy.146
  346.1 2.5 copy.152
  348.7 7.3 %copy.154 = bf16[2048,1024]{1,0:T(8,128)(2,1)} copy(f32[2048,1024]{0,1:T(8,128)} %get-tuple-element.1589) | data formatting | bytes 12582912 | tf_op jit(solution)/shard_map/while | solution.py:66
  357.1 1.3 fusion.76
  358.7 4.3 broadcast.933
  363.1 30.7 %while.83 = (s32[]{:T(128)}, f32[128,4,5,128]{3,0,2,1:T(8,128)S(1)}, f32[2048,1024]{0,1:T(8,128)}, f32[128,16]{0,1:T(8,128)S(1)}, bf16[2048,512]{0,1:T(8,128)(2,...) while((s32[]{:T(128)}, ...), condition=%wide.region_25.26_spmd.clone.clone, body=%wide.region_21.25_spmd.clone.clone.sunk | while | flops 425974784 | bytes 14221625 | solution.py:66
  364.6 5.2 conditional.19
  364.6 1.0 constant_dynamic-slice_fusion.6
  367.9 2.0 fusion.63
  393.7 7.3 %copy.155 = bf16[2048,1024]{1,0:T(8,128)(2,1)} copy(f32[2048,1024]{0,1:T(8,128)} %get-tuple-element.1590) | data formatting | bytes 12582912 | tf_op jit(solution)/shard_map/while | solution.py:66
  401.1 2.2 copy.156
  403.9 1.1 copy.157
  405.0 63.6 %reduce-scatter.3.cloned.1.call-done = bf16[128,1024]{1,0:T(8,128)(2,1)} async-done(((bf16[2048,1024]{1,0:T(8,128)(2,1)}), bf16[128,1024]{1,0:T(8,128)(2,1)}) %reduce-scatter.3.cloned.1.call-update) | async-done | bytes 262160 | tf_op jit(solution)/shard_map/reduce_scatter | solution.py:217
  468.6 97.9 %reduce-scatter.5.cloned.1.call-done = bf16[128,1024]{1,0:T(8,128)(2,1)} async-done(((bf16[2048,1024]{1,0:T(8,128)(2,1)}), bf16[128,1024]{1,0:T(8,128)(2,1)}) %reduce-scatter.5.cloned.1.call-update) | async-done | bytes 262160 | tf_op jit(solution)/shard_map/reduce_scatter | solution.py:217
  566.4 1.9 maximum_bitcast_fusion
  (363 shorter events, 85.2 us)
Async XLA Ops:
  7.2 92.6 %all-gather.9.cloned.1.call-start = ((), (), s32[]{:S(2)}) async-start(), calls=%async_computation.6 | async-start | bytes 2228224 | tf_op jit(solution)/shard_map/all_gather | solution.py:128
  9.0 2.7 copy-start.5
  9.0 153.0 %all-gather.11.cloned.1.call-start = ((), (), s32[]{:S(2)}) async-start(), calls=%async_computation.7 | async-start | bytes 2228224 | tf_op jit(solution)/shard_map/all_gather | solution.py:214
  10.8 280.2 %all-gather.13.cloned.1.call-start = ((), (), s32[]{:S(2)}) async-start(), calls=%async_computation.8 | async-start | bytes 2228224 | tf_op jit(solution)/shard_map/all_gather | solution.py:128
  13.5 12.3 %copy-start.8 = (s32[2,1,16]{2,1,0:T(1,128)S(1)}, s32[2,1,16]{2,1,0:T(1,128)}, u32[]{:S(2)}) copy-start(s32[2,1,16]{2,1,0:T(1,128)} %param.29) | copy-start | bytes 388
  13.5 12.3 %copy-start.9 = (s32[2,1,16,16]{3,2,1,0:T(8,128)S(1)}, s32[2,1,16,16]{3,2,1,0:T(8,128)}, u32[]{:S(2)}) copy-start(s32[2,1,16,16]{3,2,1,0:T(8,128)} %param.28) | copy-start | bytes 6148
  13.5 13.5 %copy-start.6 = (bf16[1,128,2560]{2,1,0:T(8,128)(2,1)S(1)}, bf16[1,128,2560]{2,1,0:T(8,128)(2,1)}, u32[]{:S(2)}) copy-start(bf16[1,128,2560]{2,1,0:T(8,128)(2,1)} %param.26) | copy-start | bytes 1966084
  13.5 192.0 %all-to-all-start = ((bf16[16,128,512]{1,2,0:T(8,128)(2,1)}), bf16[16,128,512]{1,2,0:T(8,128)(2,1)}, u32[]{:S(2)}, u32[]{:S(2)}) async-start(bf16[16,128,512]{1,2,0:T(8,128)(2,1)} %stack.15), calls=%async_computation | async-start | bytes 4194304 | tf_op jit(solution)/shard_map/all_to_all | solution.py:212
  24.9 2.5 copy-start.7
  24.9 288.6 %all-gather.15.cloned.1.call-start = ((), (), s32[]{:S(2)}) async-start(), calls=%async_computation.9 | async-start | bytes 2228224 | tf_op jit(solution)/shard_map/all_gather | solution.py:214
  204.0 1.5 copy-start.4
  207.2 136.1 %all-to-all-start.1 = ((bf16[16,128,512]{1,2,0:T(8,128)(2,1)}), bf16[16,128,512]{1,2,0:T(8,128)(2,1)}, u32[]{:S(2)}, u32[]{:S(2)}) async-start(bf16[16,128,512]{1,2,0:T(8,128)(2,1)} %stack.16), calls=%async_computation.1 | async-start | bytes 4194304 | tf_op jit(solution)/shard_map/all_to_all | solution.py:212
  226.0 242.5 %reduce-scatter.3.cloned.1.call-start = ((), (), s32[]{:S(2)}) async-start(), calls=%async_computation.4 | async-start | bytes 4456448 | tf_op jit(solution)/shard_map/reduce_scatter | solution.py:217
  230.0 4.1 copy-start.2
  286.5 27.1 %copy-start = (bf16[128,4,5,128]{3,0,2,1:T(8,128)(2,1)S(1)}, bf16[128,4,5,128]{3,0,2,1:T(8,128)(2,1)}, u32[]{:S(2)}) copy-start(bf16[128,4,5,128]{3,0,2,1:T(8,128)(2,1)} %copy.149) | copy-start | bytes 1966084
  288.9 67.2 %collective-permute-start = (bf16[128,2560]{0,1:T(8,128)(2,1)}, bf16[128,2560]{0,1:T(8,128)(2,1)}, u32[]{:S(2)}, u32[]{:S(2)}) collective-permute-start(bf16[128,2560]{0,1:T(8,128)(2,1)} %bitcast.65), channel_id=1, source_target_pairs={{16,0},{32,16},{48,32},{64,48},{80,64},{96,80},{112,96},{128,112},... | collective-permute-start | bytes 1966088 | tf_op jit(solution)/shard_map/ppermute | solution.py:18
  356.0 1.1 copy-start.3
  356.0 2.3 copy-start.1
  356.0 210.4 %reduce-scatter.5.cloned.1.call-start = ((), (), s32[]{:S(2)}) async-start(), calls=%async_computation.5 | async-start | bytes 4456448 | tf_op jit(solution)/shard_map/reduce_scatter | solution.py:217
Sparse Core Ops, SparseCore 0:
  11.0 88.7 all-gather.8
  102.2 59.7 all-gather.10
  164.4 59.7 all-gather.12
  226.5 86.9 all-gather.14
  356.2 112.3 reduce-scatter.2
  472.0 94.3 reduce-scatter.4
